TPU v7x, 256 devices: a whole 4x4x8 slice. The times are simulated.
256 devices in a mesh: gx: 8 (over z), gy: 16 (over x, y_hi, core), layer: 2 (over y_lo).
Axes of the slice: x: 4, y: 4 (y_hi: 2, y_lo: 2; y = y_hi * 2 + y_lo), z: 8, core: 2. Of those that a mesh axis runs over, the one named last changes fastest.
Arguments:
- atom_feats: bfloat16 [16384, 128], P(('gx', 'gy', 'layer')), may hold values from -6 to 6
- bond_embed: bfloat16 [589824, 128], P(('gx', 'gy', 'layer')), may hold values from -6 to 6
- pair_dist: float32 [1179648], P(('gx', 'gy', 'layer')), may hold values from 1.4 to 6.9
- neighbours: int32 [1179648], P(('gx', 'gy', 'layer')), may hold values from 0 to 1151, as said below
- slot_kind: int32 [1179648], P(('gx', 'gy', 'layer')), may hold values from 0 to 2
- own_rows: int32 [589824], P(('gx', 'gy', 'layer')), may hold values from 0 to 4607, as said below
- send_pos: int32 [589824], P(('gx', 'gy', 'layer')), may hold values from 0 to 2303, as said below
- recv_pos: int32 [1179648], P(('gx', 'gy', 'layer')), may hold values from 0 to 2303, as said below
- w_left: bfloat16 [3, 128, 128], replicated, may hold values from -0.5 to 0.5
- w_right: bfloat16 [3, 128, 128], replicated, may hold values from -0.5 to 0.5
- w_edge_in: bfloat16 [3, 128, 128], replicated, may hold values from -0.5 to 0.5
- w_edge_out: bfloat16 [3, 128, 128], replicated, may hold values from -0.5 to 0.5
- w_msg: bfloat16 [2, 128, 128], replicated, may hold values from -0.5 to 0.5
- w_upd: bfloat16 [2, 128, 128], replicated, may hold values from -0.5 to 0.5
- node_gain: float32 [2, 128], replicated, may hold values from 0.1 to 1.9
- w_block: bfloat16 [128, 169], replicated, may hold values from -0.5 to 0.5
Outputs:
- blocks: bfloat16 [169, 1179648], P(None, ('gx', 'gy', 'layer'))
Inputs may be any that keep to these rules, and one draw needn't show every extreme that they name: `neighbours`: slots pair up: a slot of kind 1 or 2 and the slot of its partner atom that points back form one pair, one of kind 1 and the other of kind 2, with equal distance; empty slots pair with empty slots. Each atom has 4 slots towards each of the 18 offsets, half of them owned. `own_rows`: each domain's rows list its 2304 owned slots once each; the valid ones (kind 1) come first, at most 2112 of them, and some domain has exactly 2112. `send_pos`: within a domain every value occurs once; value // 128 is the offset of the partner's domain. `recv_pos`: for slots of kind 2: value // 128 is the reverse of the offset of the partner's domain.
All inputs are finite; a program needn't handle non-finite values.
Results may differ from a plain program's by a relative error of at most 0.019.
Values may be sent and summed in bfloat16 or wider, within the bound.
A program may use at most 64 MiB of HBM per device.

v0:
```python
import jax
import jax.numpy as jnp
from jax import lax
from jax.experimental import pallas as pl
from jax.experimental.pallas import tpu as pltpu
from jax.sharding import PartitionSpec as P

ORB = 13
LAYERS = 3
OFFSETS = 18
SELF = 4
ATOMS = 64
NEIGH = 72
SLOTS = ATOMS * NEIGH
CAP = 128
LISTED = 2176
MESH = pl.DeviceIdType.MESH
BF = jnp.bfloat16
F32 = jnp.float32
NT = (((1,), (1,)), ((), ()))


def dot(a, b):
    return jnp.dot(a, b, preferred_element_type=F32)


def dot_nt(a, b):
    return lax.dot_general(a, b, NT, preferred_element_type=F32)


def silu(v):
    half = 0.5 * v
    return half + half * jnp.tanh(half)


def reverse_of(offset):
    return offset // 9 * 9 + 8 - offset % 9


def kernel(
    atom_ref,
    bond_ref,
    slot_ref,
    dist_ref,
    owned_ref,
    wl_ref,
    wr_ref,
    wi_ref,
    wo_ref,
    wm_ref,
    wu_ref,
    gain_ref,
    wb_ref,
    out_ref,
    ghost,
    hidden,
    bond_send,
    bond_recv,
    rows,
    pick_far,
    mix,
    tables,
    message,
    edge,
    last,
    wide,
    place,
    spread,
    blocks,
    send_sem,
    recv_sem,
):
    gx, gy, sheet = lax.axis_index("gx"), lax.axis_index("gy"), lax.axis_index("layer")
    n_gx, n_gy = lax.axis_size("gx"), lax.axis_size("gy")

    def partner(offset):
        step_x = offset % 9 // 3 - 1
        step_y = offset % 3 - 1
        return (
            (gx + step_x + n_gx) % n_gx,
            (gy + step_y + n_gy) % n_gy,
            (sheet + offset // 9) % 2,
        )

    others = [o for o in range(OFFSETS) if o != SELF]

    barrier = pltpu.get_barrier_semaphore()
    for o in others:
        pl.semaphore_signal(barrier, inc=1, device_id=partner(o), device_id_type=MESH)
    pl.semaphore_wait(barrier, len(others))

    def ghost_copy(layer, o):
        source = atom_ref if layer == 0 else hidden.at[layer - 1]
        return pltpu.make_async_remote_copy(
            src_ref=source,
            dst_ref=ghost.at[layer, reverse_of(o)],
            send_sem=send_sem.at[layer, o],
            recv_sem=recv_sem.at[layer, reverse_of(o)],
            device_id=partner(o),
            device_id_type=MESH,
        )

    def bond_copy(o):
        return pltpu.make_async_remote_copy(
            src_ref=bond_send.at[o],
            dst_ref=bond_recv.at[reverse_of(o)],
            send_sem=send_sem.at[3, o],
            recv_sem=recv_sem.at[3, reverse_of(o)],
            device_id=partner(o),
            device_id_type=MESH,
        )

    for o in others:
        ghost_copy(0, o).start()
    ghost[0, SELF] = atom_ref[...]

    slot = slot_ref[...]
    nbr, kind, place_in = slot & 2047, (slot >> 11) & 3, slot >> 13
    offset_of = nbr >> 6
    atom_of = ((nbr & 63) + 1).astype(F32)
    scaled = dist_ref[...] / 7.0
    falloff = 1.0 - scaled * scaled
    env = jnp.where(kind > 0, falloff * falloff, 0.0)
    own_key = jnp.where(kind == 1, offset_of, -1)
    far_key = jnp.where(kind == 2, offset_of, -1)
    recv_place = (place_in + 1).astype(F32)

    sub72 = lax.broadcasted_iota(jnp.int32, (NEIGH, 128), 0)
    sub = lax.broadcasted_iota(jnp.int32, (128, 128), 0)
    lane = lax.broadcasted_iota(jnp.int32, (128, 128), 1)

    send_place = jnp.zeros((NEIGH, 128), F32)
    for k in range(OFFSETS):
        owned = owned_ref[k : k + 1, :]
        at_slot = jnp.where(((owned >> 6) & 127) == sub72, 1.0, 0.0).astype(BF)
        value = (((owned >> 13) & 127) + 1).astype(F32)
        at_atom = jnp.where((owned & 63) == (sub & 63), value, 0.0).astype(BF)
        send_place = send_place + dot_nt(at_slot, at_atom)

    before = jnp.where(
        lax.broadcasted_iota(jnp.int32, (NEIGH, NEIGH), 0)
        > lax.broadcasted_iota(jnp.int32, (NEIGH, NEIGH), 1),
        1.0,
        0.0,
    ).astype(BF)
    rank_lane = (lax.broadcasted_iota(jnp.int32, (NEIGH, 128), 1) >> 6).astype(F32)

    def total(v):
        return jnp.sum(v, axis=0, keepdims=True)

    def tables_step(o, where_to):
        own = jnp.where(own_key == o, 1.0, 0.0)
        far = jnp.where(far_key == o, 1.0, 0.0)
        count = dot(before, jnp.concatenate([own, far], axis=1).astype(BF))
        own_rank, far_rank = count[:, :128], count[:, 128:]
        own_hit = jnp.where(own_rank == rank_lane, own, 0.0)
        far_hit = jnp.where(far_rank == rank_lane, far, 0.0)
        rows[0, pl.ds(o, 1), :] = total(own_hit * atom_of) - 1.0
        rows[1, pl.ds(o, 1), :] = total(far_hit * atom_of) - 1.0
        rows[2, pl.ds(o, 1), :] = total(own_hit * send_place) - 1.0
        rows[3, pl.ds(o, 1), :] = total(far_hit * recv_place) - 1.0
        rows[4, pl.ds(o, 1), :] = total(own_hit * env)
        rows[5, pl.ds(o, 1), :] = total(far_hit * env)
        base = (4 * o + 1).astype(F32)
        return where_to + own * (own_rank + base) + far * (far_rank + (base + 2.0))

    where_to = lax.fori_loop(0, OFFSETS, tables_step, jnp.zeros((NEIGH, 128), F32))

    subf = (sub & 63).astype(F32)
    for g in range(OFFSETS // 2):
        low = sub < 64

        def pair(kind_of_row):
            first = rows[kind_of_row, 2 * g : 2 * g + 1, :]
            second = rows[kind_of_row, 2 * g + 1 : 2 * g + 2, :]
            return jnp.where(low, first, second)

        weights = jnp.where(pair(0) == subf, pair(4), 0.0) + jnp.where(
            pair(1) == subf, pair(5), 0.0
        )
        mix[:, g * 128 : (g + 1) * 128] = weights.T.astype(BF)

    sub384 = lax.broadcasted_iota(jnp.int32, (384, 128), 0)

    def bond_step(step, carry):
        first = step * 384
        picked = [
            jnp.where((owned_ref[k : k + 1, :] >> 13) - first == sub384, 1.0, 0.0).astype(BF)
            for k in range(LISTED // 128)
        ]
        got = dot(jnp.concatenate(picked, axis=1), bond_ref[:LISTED, :]).astype(BF)
        for i in range(3):
            o = step * 3 + i
            bond_send[o] = got[i * 128 : (i + 1) * 128, :]

            @pl.when(o != SELF)
            def _():
                bond_copy(o).start()

        return carry

    lax.fori_loop(0, OFFSETS // 3, bond_step, 0)

    def wait_ghost(layer):
        for o in others:
            pltpu.make_async_remote_copy(
                src_ref=ghost.at[layer, o],
                dst_ref=ghost.at[layer, o],
                send_sem=send_sem.at[layer, o],
                recv_sem=recv_sem.at[layer, o],
                device_id=partner(o),
                device_id_type=MESH,
            ).wait_recv()

    def update_hidden(layer):
        ghosts = ghost[layer].reshape(OFFSETS * ATOMS, 128)
        message[...] = dot(ghosts, wm_ref[layer]).astype(BF)
        two = dot(mix[...], message[...])
        summed = ((two[:ATOMS] + two[ATOMS:]) * 0.125).astype(BF)
        updated = ghost[layer, SELF].astype(F32) + silu(dot(summed, wu_ref[layer]))
        mean = jnp.mean(updated * updated, axis=-1, keepdims=True)
        fresh = updated * lax.rsqrt(mean + 1e-06) * gain_ref[layer : layer + 1, :]
        hidden[layer] = fresh.astype(BF)
        for o in others:
            ghost_copy(layer + 1, o).start()
        ghost[layer + 1, SELF] = fresh.astype(BF)

    def project(layer):
        both = jnp.concatenate([wr_ref[layer], wl_ref[layer]], axis=1)

        def one(o, carry):
            got = dot(ghost[layer, o], both).astype(BF)
            tables[o, 0:64, 0:128] = got[:, :128]
            tables[o, 64:128, 128:256] = got[:, 128:]
            return carry

        lax.fori_loop(0, OFFSETS, one, 0)

    ones = jnp.full((128, 128), 1.0 / 128.0, BF)

    def edge_layer(layer, final):
        right = tables[SELF, 0:64, 0:128].astype(F32)
        left = tables[SELF, 64:128, 128:256].astype(F32)
        left2 = jnp.concatenate([left, left], axis=0)
        right2 = jnp.concatenate([right, right], axis=0)
        edge_in, edge_out = wi_ref[layer], wo_ref[layer]

        def one(o, carry):
            state = edge[o]
            reached = dot(pick_far[o], tables[o])
            product = jnp.concatenate(
                [reached[:, :128] * left2, reached[:, 128:] * right2], axis=0
            )
            gate = silu(dot(state, edge_in) * product).astype(BF)
            renewed = state.astype(F32) + dot(gate, edge_out)
            mean = jnp.mean(renewed * renewed, axis=-1, keepdims=True)
            fresh = renewed * lax.rsqrt(mean + 1e-06)
            if final:
                last[pl.ds(o * 256, 256), :] = fresh
            else:
                edge[o] = fresh.astype(BF)
            return carry

        lax.fori_loop(0, OFFSETS, one, 0)

    wait_ghost(0)
    update_hidden(0)

    tables[...] = jnp.zeros_like(tables)

    def far_step(o, carry):
        own_atom, far_atom = rows[0, pl.ds(o, 1), :], rows[1, pl.ds(o, 1), :]
        wanted = jnp.where(sub < 64, own_atom, far_atom)
        pick_far[o] = jnp.where(wanted == subf, 1.0, 0.0).T.astype(BF)
        return carry

    lax.fori_loop(0, OFFSETS, far_step, 0)
    project(0)

    subq = sub.astype(F32)

    def own_step(o, carry):
        wanted = rows[2, pl.ds(o, 1), :]
        picker = jnp.where(wanted == subq, 1.0, 0.0).T.astype(BF)
        edge[o, 0:128, :] = dot(picker, bond_send[o]).astype(BF)
        return carry

    lax.fori_loop(0, OFFSETS, own_step, 0)

    for n in range(ATOMS):
        spread[n * NEIGH : (n + 1) * NEIGH, :] = jnp.broadcast_to(
            where_to[:, n : n + 1], (NEIGH, 128)
        ) + jnp.where(
            jnp.broadcast_to(where_to[:, n : n + 1], (NEIGH, 128)) > 0.0, n * 72.0 - 1.0, -1.0
        )

    def place_step(i, carry):
        start = jnp.clip(i * 256 - 128, 0, SLOTS - 512)
        column = spread[pl.ds(pl.multiple_of(i * 256, 256), 256), :]
        for k in range(4):
            here = (lax.broadcasted_iota(jnp.int32, (256, 128), 1) + (start + k * 128)).astype(F32)
            place[i, :, k * 128 : (k + 1) * 128] = jnp.where(column == here, 1.0, 0.0).astype(BF)
        return carry

    lax.fori_loop(0, SLOTS // 256, place_step, 0)

    for o in others:
        pltpu.make_async_remote_copy(
            src_ref=bond_recv.at[o],
            dst_ref=bond_recv.at[o],
            send_sem=send_sem.at[3, o],
            recv_sem=recv_sem.at[3, o],
            device_id=partner(o),
            device_id_type=MESH,
        ).wait_recv()
    bond_recv[SELF] = bond_send[SELF]

    def recv_step(o, carry):
        wanted = rows[3, pl.ds(o, 1), :]
        picker = jnp.where(wanted == subq, 1.0, 0.0).T.astype(BF)
        edge[o, 128:256, :] = dot(picker, bond_recv[o]).astype(BF)
        return carry

    lax.fori_loop(0, OFFSETS, recv_step, 0)
    edge_layer(0, False)

    wait_ghost(1)
    update_hidden(1)
    project(1)
    edge_layer(1, False)

    row = lax.broadcasted_iota(jnp.int32, (ORB * ORB, ORB * ORB), 0)
    col = lax.broadcasted_iota(jnp.int32, (ORB * ORB, ORB * ORB), 1)
    coarse = jnp.floor((row.astype(F32) + 0.5) * (1.0 / ORB))
    source = (row.astype(F32) - coarse * ORB) * ORB + coarse
    keep = jnp.where(row == col, 1.0, 0.0).astype(BF)
    swap = jnp.where(source == col.astype(F32), 1.0, 0.0).astype(BF)
    block_map = jnp.concatenate(
        [dot_nt(keep, wb_ref[...]), dot_nt(swap, wb_ref[...])], axis=1
    ).astype(BF)

    wait_ghost(2)
    project(2)
    edge_layer(2, True)

    is_own = (lax.broadcasted_iota(jnp.int32, (NEIGH, 128), 0) & 2) == 0

    def widen(m, carry):
        halves = []
        for i in range(2):
            mine = last[pl.ds(2 * m + i, NEIGH, stride=ATOMS), :]
            halves.append(
                jnp.concatenate([jnp.where(is_own, mine, 0.0), jnp.where(is_own, 0.0, mine)], axis=1)
            )
        wide[pl.ds(pl.multiple_of(m * 144, 144), 144), :] = jnp.concatenate(halves, axis=0).astype(BF)
        return carry

    lax.fori_loop(0, ATOMS // 2, widen, 0)

    def block_step(c, carry):
        at = pl.multiple_of(c * 512, 512)
        blocks[:, pl.ds(at, 512)] = dot_nt(block_map, wide[pl.ds(at, 512), :]).astype(BF)
        return carry

    lax.fori_loop(0, SLOTS // 512, block_step, 0)

    def out_step(i, carry):
        start = pl.multiple_of(jnp.clip(i * 256 - 128, 0, SLOTS - 512), 128)
        at = pl.multiple_of(i * 256, 256)
        out_ref[:, pl.ds(at, 256)] = dot_nt(blocks[:, pl.ds(start, 512)], place[i]).astype(BF)
        return carry

    lax.fori_loop(0, SLOTS // 256, out_step, 0)

    for layer in range(LAYERS):
        for o in others:
            ghost_copy(layer, o).wait_send()
    for o in others:
        bond_copy(o).wait_send()


def shards(
    atom_feats,
    bond_embed,
    pair_dist,
    neighbours,
    slot_kind,
    own_rows,
    send_pos,
    recv_pos,
    w_left,
    w_right,
    w_edge_in,
    w_edge_out,
    w_msg,
    w_upd,
    node_gain,
    w_block,
):
    slots = neighbours | (slot_kind << 11) | ((recv_pos & 127) << 13)
    slots = jnp.tile(slots.reshape(ATOMS, NEIGH).T, (1, 2))
    dist = jnp.tile(pair_dist.reshape(ATOMS, NEIGH).T, (1, 2))
    owned = (own_rows // NEIGH) | ((own_rows % NEIGH) << 6) | (send_pos << 13)
    owned = owned.reshape(OFFSETS, 128)
    vmem = pl.BlockSpec(memory_space=pltpu.VMEM)
    return pl.pallas_call(
        kernel,
        out_shape=jax.ShapeDtypeStruct((ORB * ORB, SLOTS), BF),
        in_specs=[vmem] * 13,
        out_specs=vmem,
        scratch_shapes=[
            pltpu.VMEM((LAYERS, OFFSETS, ATOMS, 128), BF),
            pltpu.VMEM((LAYERS - 1, ATOMS, 128), BF),
            pltpu.VMEM((OFFSETS, CAP, 128), BF),
            pltpu.VMEM((OFFSETS, CAP, 128), BF),
            pltpu.VMEM((6, 24, 128), F32),
            pltpu.VMEM((OFFSETS, 128, 128), BF),
            pltpu.VMEM((128, OFFSETS * ATOMS), BF),
            pltpu.VMEM((OFFSETS, 128, 256), BF),
            pltpu.VMEM((OFFSETS * ATOMS, 128), BF),
            pltpu.VMEM((OFFSETS, 256, 128), BF),
            pltpu.VMEM((SLOTS, 128), F32),
            pltpu.VMEM((SLOTS, 256), BF),
            pltpu.VMEM((SLOTS // 256, 256, 512), BF),
            pltpu.VMEM((SLOTS, 128), F32),
            pltpu.VMEM((ORB * ORB, SLOTS), BF),
            pltpu.SemaphoreType.DMA((4, OFFSETS)),
            pltpu.SemaphoreType.DMA((4, OFFSETS)),
        ],
        compiler_params=pltpu.CompilerParams(
            collective_id=0, has_side_effects=True, vmem_limit_bytes=48 << 20
        ),
    )(
        atom_feats,
        bond_embed,
        slots,
        dist,
        owned,
        w_left,
        w_right,
        w_edge_in,
        w_edge_out,
        w_msg,
        w_upd,
        node_gain,
        w_block,
    )


def solution(mesh):
    spread = ("gx", "gy", "layer")
    placed = (P(spread, None), P(spread, None)) + (P(spread),) * 6 + (P(),) * 8
    return jax.shard_map(
        shards, mesh=mesh, in_specs=placed, out_specs=P(None, spread), check_vma=False
    )
```

profile of v0, /device:TPU:1, one launch (start us, length us, event | category | flops | bytes accessed | tf_op | source)
XLA Modules:
  0.0 83.2 jit_solution(11075528436086134836)
XLA Ops:
  0.0 0.7 fusion.2.owned_ref
  0.7 0.8 shift-left_or_fusion
  1.5 0.1 reshape.17
  1.6 0.1 copy.18
  1.7 0.8 reshape.18
  2.5 0.1 copy.19
  2.6 0.1 tile.21.dist_ref
  2.8 0.1 tile.9.slot_ref
  2.9 0.9 %copy.20.wb_ref = bf16[128,169]{1,0:T(8,128)(2,1)S(1)} copy(bf16[128,169]{0,1:T(8,128)(2,1)} %param.31) | data formatting | bytes 86528 | tf_op args[15]
  3.8 0.0 copy-start
  3.8 1.1 %copy-done = bf16[2304,128]{1,0:T(8,128)(2,1)S(1)} copy-done((bf16[2304,128]{1,0:T(8,128)(2,1)S(1)}, bf16[2304,128]{1,0:T(8,128)(2,1)}, u32[]{:S(2)}) %copy-start) | copy-done | bytes 589848
  4.8 0.0 copy-start.1
  4.8 0.9 %copy-done.1 = bf16[3,128,128]{2,1,0:T(8,128)(2,1)S(1)} copy-done((bf16[3,128,128]{2,1,0:T(8,128)(2,1)S(1)}, bf16[3,128,128]{2,1,0:T(8,128)(2,1)}, u32[]{:S(2)}) %copy-start.1) | copy-done | bytes 98328
  5.7 0.0 copy-start.2
  5.7 0.9 %copy-done.2 = bf16[3,128,128]{2,1,0:T(8,128)(2,1)S(1)} copy-done((bf16[3,128,128]{2,1,0:T(8,128)(2,1)S(1)}, bf16[3,128,128]{2,1,0:T(8,128)(2,1)}, u32[]{:S(2)}) %copy-start.2) | copy-done | bytes 98328
  6.6 0.9 %copy-done.3 = bf16[3,128,128]{2,1,0:T(8,128)(2,1)S(1)} copy-done((bf16[3,128,128]{2,1,0:T(8,128)(2,1)S(1)}, bf16[3,128,128]{2,1,0:T(8,128)(2,1)}, u32[]{:S(2)}) %copy-start.3) | copy-done | bytes 98328
  7.5 0.0 copy-start.4
  7.5 0.9 %copy-done.4 = bf16[3,128,128]{2,1,0:T(8,128)(2,1)S(1)} copy-done((bf16[3,128,128]{2,1,0:T(8,128)(2,1)S(1)}, bf16[3,128,128]{2,1,0:T(8,128)(2,1)}, u32[]{:S(2)}) %copy-start.4) | copy-done | bytes 98328
  8.4 0.8 %copy-done.5 = bf16[2,128,128]{2,1,0:T(8,128)(2,1)S(1)} copy-done((bf16[2,128,128]{2,1,0:T(8,128)(2,1)S(1)}, bf16[2,128,128]{2,1,0:T(8,128)(2,1)}, u32[]{:S(2)}) %copy-start.5) | copy-done | bytes 65560
  9.2 0.8 %copy-done.6 = bf16[2,128,128]{2,1,0:T(8,128)(2,1)S(1)} copy-done((bf16[2,128,128]{2,1,0:T(8,128)(2,1)S(1)}, bf16[2,128,128]{2,1,0:T(8,128)(2,1)}, u32[]{:S(2)}) %copy-start.6) | copy-done | bytes 65560
  10.1 0.7 copy-done.7
  10.8 0.7 copy-done.8
  11.5 70.5 %shard_map.154 = bf16[169,4608]{1,0:T(8,128)(2,1)S(1)} custom-call(bf16[64,128]{1,0:T(8,128)(2,1)S(1)} %copy-done.7, bf16[2304,128]{1,0:T(8,128)(2,1)S(1)} %copy-done, s32[72,128]{1,0:T(8,128)S(1)} %tile.9.slot_ref, f32[72,128]{1,0:T(8,128)S(1)} %tile.21.dist_ref, s32[18,128]{1,0:T(8,128)S(1)} %fusion.2.owned_ref, bf16[3,128,128]{2,1,0:T(8,128)(2,1)S(1)} %copy-done.1, ...), custom_call_target="tpu_custom_call" | custom-call | tf_op jit(solution)/shard_map/pallas_call | solution.py:406
  82.0 1.2 %copy.22 = bf16[169,4608]{1,0:T(8,128)(2,1)} copy(bf16[169,4608]{1,0:T(8,128)(2,1)S(1)} %shard_map.154) | data formatting | bytes 3115008
  (7 shorter events, 0.1 us)
Async XLA Ops:
  3.8 1.1 %copy-start = (bf16[2304,128]{1,0:T(8,128)(2,1)S(1)}, bf16[2304,128]{1,0:T(8,128)(2,1)}, u32[]{:S(2)}) copy-start(bf16[2304,128]{1,0:T(8,128)(2,1)} %bond_ref.1) | copy-start | bytes 1769476
  4.8 0.9 %copy-start.1 = (bf16[3,128,128]{2,1,0:T(8,128)(2,1)S(1)}, bf16[3,128,128]{2,1,0:T(8,128)(2,1)}, u32[]{:S(2)}) copy-start(bf16[3,128,128]{2,1,0:T(8,128)(2,1)} %wl_ref.1) | copy-start | bytes 294916
  5.7 0.9 %copy-start.2 = (bf16[3,128,128]{2,1,0:T(8,128)(2,1)S(1)}, bf16[3,128,128]{2,1,0:T(8,128)(2,1)}, u32[]{:S(2)}) copy-start(bf16[3,128,128]{2,1,0:T(8,128)(2,1)} %wr_ref.1) | copy-start | bytes 294916
  6.6 0.9 %copy-start.3 = (bf16[3,128,128]{2,1,0:T(8,128)(2,1)S(1)}, bf16[3,128,128]{2,1,0:T(8,128)(2,1)}, u32[]{:S(2)}) copy-start(bf16[3,128,128]{2,1,0:T(8,128)(2,1)} %wi_ref.1) | copy-start | bytes 294916
  7.5 0.9 %copy-start.4 = (bf16[3,128,128]{2,1,0:T(8,128)(2,1)S(1)}, bf16[3,128,128]{2,1,0:T(8,128)(2,1)}, u32[]{:S(2)}) copy-start(bf16[3,128,128]{2,1,0:T(8,128)(2,1)} %wo_ref.1) | copy-start | bytes 294916
  8.4 0.8 %copy-start.5 = (bf16[2,128,128]{2,1,0:T(8,128)(2,1)S(1)}, bf16[2,128,128]{2,1,0:T(8,128)(2,1)}, u32[]{:S(2)}) copy-start(bf16[2,128,128]{2,1,0:T(8,128)(2,1)} %wm_ref.1) | copy-start | bytes 196612
  9.2 0.8 %copy-start.6 = (bf16[2,128,128]{2,1,0:T(8,128)(2,1)S(1)}, bf16[2,128,128]{2,1,0:T(8,128)(2,1)}, u32[]{:S(2)}) copy-start(bf16[2,128,128]{2,1,0:T(8,128)(2,1)} %wu_ref.1) | copy-start | bytes 196612
  10.1 0.7 copy-start.7
  10.8 0.7 copy-start.8
where the time goes:
time: 83.8 us; the launch traced here: 83.2 us
  Pallas kernels  70.5 us (84%)
  local copies, waits for them, and re-layouts  11.1 us (13%)
  other arithmetic  1.51 us (2%)
    pallas_call x1, Pallas kernels, shards(): pl.pallas_call(kernel, out_shape=jax.ShapeDtypeStruct((ORB * ORB, SLOTS),...  70.5 us
    unnamed x20, local copies, waits for them, and re-layouts  9.75 us

commit v1 on v0

v1 whole, which is shorter than its diff:
```python
import jax
import jax.numpy as jnp
from jax import lax
from jax.experimental import pallas as pl
from jax.experimental.pallas import tpu as pltpu
from jax.sharding import PartitionSpec as P

ORB = 13
LAYERS = 3
OFFSETS = 18
SELF = 4
ATOMS = 64
NEIGH = 72
SLOTS = ATOMS * NEIGH
CAP = 128
LISTED = 2176
GROUP = 3
UNROLL = 1
MESH = pl.DeviceIdType.MESH
BF = jnp.bfloat16
F32 = jnp.float32
NT = (((1,), (1,)), ((), ()))


def dot(a, b):
    return jnp.dot(a, b, preferred_element_type=F32)


def dot_nt(a, b):
    return lax.dot_general(a, b, NT, preferred_element_type=F32)


def silu(v):
    half = 0.5 * v
    return half + half * jnp.tanh(half)


def reverse_of(offset):
    return offset // 9 * 9 + 8 - offset % 9


def kernel(
    *refs,
):
    sources, out_ref, held = refs[:16], refs[16], refs[17:33]
    (
        ghost,
        hidden,
        bond_send,
        bond_recv,
        line,
        rows,
        flat,
        pick_far,
        mix,
        tables,
        edge,
        last,
        wide,
        turned,
        place,
        blocks,
        in_sem,
        out_sem,
        send_sem,
        recv_sem,
    ) = refs[33:]
    (
        atom_ref,
        bond_ref,
        dist_ref,
        nbr_ref,
        kind_ref,
        own_ref,
        send_ref,
        recv_ref,
        wl_ref,
        wr_ref,
        wi_ref,
        wo_ref,
        wm_ref,
        wu_ref,
        gain_ref,
        wb_ref,
    ) = held
    gx, gy, sheet = lax.axis_index("gx"), lax.axis_index("gy"), lax.axis_index("layer")
    n_gx, n_gy = lax.axis_size("gx"), lax.axis_size("gy")

    def partner(offset):
        step_x = offset % 9 // 3 - 1
        step_y = offset % 3 - 1
        return (
            (gx + step_x + n_gx) % n_gx,
            (gy + step_y + n_gy) % n_gy,
            (sheet + offset // 9) % 2,
        )

    others = [0, 2, 6, 8, 9, 11, 15, 17, 3, 5, 12, 14, 1, 7, 10, 16, 13]

    barrier = pltpu.get_barrier_semaphore()
    for o in others:
        pl.semaphore_signal(barrier, inc=1, device_id=partner(o), device_id_type=MESH)
    fetches = [
        pltpu.make_async_copy(source, target, in_sem.at[i])
        for i, (source, target) in enumerate(zip(sources, held))
    ]
    for i in (5, 6, 3, 4, 7, 2, 0, 1, 12, 13, 14, 8, 9, 10, 11, 15):
        fetches[i].start()
    def ghost_copy(layer, o):
        source = atom_ref if layer == 0 else hidden.at[layer - 1]
        return pltpu.make_async_remote_copy(
            src_ref=source,
            dst_ref=ghost.at[layer, reverse_of(o)],
            send_sem=send_sem.at[layer, o],
            recv_sem=recv_sem.at[layer, reverse_of(o)],
            device_id=partner(o),
            device_id_type=MESH,
        )

    def bond_copy(o):
        return pltpu.make_async_remote_copy(
            src_ref=bond_send.at[o],
            dst_ref=bond_recv.at[reverse_of(o)],
            send_sem=send_sem.at[3, o],
            recv_sem=recv_sem.at[3, reverse_of(o)],
            device_id=partner(o),
            device_id_type=MESH,
        )

    for i in (5, 6, 3, 4, 7, 2):
        fetches[i].wait()

    sub = lax.broadcasted_iota(jnp.int32, (128, 128), 0)
    lane1 = lax.broadcasted_iota(jnp.int32, (1, 128), 1)
    packed = (nbr_ref[...] | (kind_ref[...] << 11) | ((recv_ref[...] & 127) << 13)).astype(F32)
    flat[0 : SLOTS // 128, :] = packed

    def by_slot(source, k):
        for n in range(ATOMS):
            at, first = n * NEIGH // 128, n * NEIGH % 128
            mine = source[at : at + 1, :]
            if first + NEIGH > 128:
                mine = jnp.where(lane1 >= first, mine, source[at + 1 : at + 2, :])
            line[k, n : n + 1, :] = mine
        moved = jnp.concatenate([line[k], line[k]], axis=0)
        for bit in (1, 2, 4, 8):
            moved = jnp.where((sub * 7 & bit) != 0, pltpu.roll(moved, 8 * bit, 1), moved)
        return moved.T[:NEIGH, :]

    slot = by_slot(flat, 0).astype(jnp.int32)
    nbr, kind, place_in = slot & 2047, (slot >> 11) & 3, slot >> 13
    offset_of = nbr >> 6
    atom_of = ((nbr & 63) + 1).astype(F32)
    scaled = by_slot(dist_ref, 1) / 7.0
    falloff = 1.0 - scaled * scaled
    env = jnp.where(kind > 0, falloff * falloff, 0.0)
    own_key = jnp.where(kind == 1, offset_of, -1)
    far_key = jnp.where(kind == 2, offset_of, -1)
    recv_place = (place_in + 1).astype(F32)

    sub72 = lax.broadcasted_iota(jnp.int32, (NEIGH, 128), 0)
    send_place = jnp.zeros((NEIGH, 128), F32)
    own_rows = own_ref[...].astype(F32)
    own_atom = jnp.floor((own_rows + 0.5) * (1.0 / NEIGH))
    own_slot = own_rows - own_atom * NEIGH
    own_place = ((send_ref[...] & 127) + 1).astype(F32)
    sub_slot, sub_atom = sub72.astype(F32), (sub & 63).astype(F32)
    for k in range(OFFSETS):
        at_slot = jnp.where(own_slot[k : k + 1, :] == sub_slot, 1.0, 0.0).astype(BF)
        at_atom = jnp.where(own_atom[k : k + 1, :] == sub_atom, own_place[k : k + 1, :], 0.0)
        send_place = send_place + dot_nt(at_slot, at_atom.astype(BF))

    before = jnp.where(
        lax.broadcasted_iota(jnp.int32, (NEIGH, NEIGH), 0)
        > lax.broadcasted_iota(jnp.int32, (NEIGH, NEIGH), 1),
        1.0,
        0.0,
    ).astype(BF)
    rank_lane = (lax.broadcasted_iota(jnp.int32, (NEIGH, 128), 1) >> 6).astype(F32)

    def total(v):
        return jnp.sum(v, axis=0, keepdims=True)

    def tables_step(o, where_to):
        own = jnp.where(own_key == o, 1.0, 0.0)
        far = jnp.where(far_key == o, 1.0, 0.0)
        count = dot(before, jnp.concatenate([own, far], axis=1).astype(BF))
        own_rank, far_rank = count[:, :128], count[:, 128:]
        own_hit = jnp.where(own_rank == rank_lane, own, 0.0)
        far_hit = jnp.where(far_rank == rank_lane, far, 0.0)
        rows[0, pl.ds(o, 1), :] = total(own_hit * atom_of) - 1.0
        rows[1, pl.ds(o, 1), :] = total(far_hit * atom_of) - 1.0
        rows[2, pl.ds(o, 1), :] = total(own_hit * send_place) - 1.0
        rows[3, pl.ds(o, 1), :] = total(far_hit * recv_place) - 1.0
        rows[4, pl.ds(o, 1), :] = total(own_hit * env)
        rows[5, pl.ds(o, 1), :] = total(far_hit * env)
        base = (4 * o + 1).astype(F32)
        return where_to + own * (own_rank + base) + far * (far_rank + (base + 2.0))

    where_to = lax.fori_loop(0, OFFSETS, tables_step, jnp.zeros((NEIGH, 128), F32), unroll=6)

    subf = (sub & 63).astype(F32)
    for g in range(OFFSETS // 2):
        low = sub < 64

        def pair(kind_of_row):
            first = rows[kind_of_row, 2 * g : 2 * g + 1, :]
            second = rows[kind_of_row, 2 * g + 1 : 2 * g + 2, :]
            return jnp.where(low, first, second)

        weights = jnp.where(pair(0) == subf, pair(4), 0.0) + jnp.where(
            pair(1) == subf, pair(5), 0.0
        )
        mix[:, g * 128 : (g + 1) * 128] = weights.T.astype(BF)

    def far_step(o, carry):
        own_atom, far_atom = rows[0, pl.ds(o, 1), :], rows[1, pl.ds(o, 1), :]
        wanted = jnp.where(sub < 64, own_atom, far_atom)
        pick_far[o] = jnp.where(wanted == subf, 1.0, 0.0).astype(BF).T
        return carry

    lax.fori_loop(0, OFFSETS, far_step, 0, unroll=6)
    fetches[0].wait()

    pl.semaphore_wait(barrier, len(others))
    for o in others:
        ghost_copy(0, o).start()
    ghost[0, SELF] = atom_ref[...]

    sub384 = lax.broadcasted_iota(jnp.int32, (384, 128), 0)

    def bond_step(step, carry):
        first = step * 384
        picked = [
            jnp.where(send_ref[k : k + 1, :] - first == sub384, 1.0, 0.0).astype(BF)
            for k in range(LISTED // 128)
        ]
        got = dot(jnp.concatenate(picked, axis=1), bond_ref[:LISTED, :]).astype(BF)
        for i in range(3):
            o = step * 3 + i
            bond_send[o] = got[i * 128 : (i + 1) * 128, :]

            @pl.when(o != SELF)
            def _():
                bond_copy(o).start()

        return carry

    fetches[1].wait()
    lax.fori_loop(0, OFFSETS // 3, bond_step, 0)

    def wait_ghost(layer):
        for o in others:
            pltpu.make_async_remote_copy(
                src_ref=ghost.at[layer, o],
                dst_ref=ghost.at[layer, o],
                send_sem=send_sem.at[layer, o],
                recv_sem=recv_sem.at[layer, o],
                device_id=partner(o),
                device_id_type=MESH,
            ).wait_recv()

    def update_hidden(layer):
        two = dot(mix[...], ghost[layer].reshape(OFFSETS * ATOMS, 128))
        reached = (two[:ATOMS] + two[ATOMS:]).astype(BF)
        summed = (dot(reached, wm_ref[layer]) * 0.125).astype(BF)
        updated = ghost[layer, SELF].astype(F32) + silu(dot(summed, wu_ref[layer]))
        mean = jnp.mean(updated * updated, axis=-1, keepdims=True)
        fresh = updated * lax.rsqrt(mean + 1e-06) * gain_ref[layer : layer + 1, :]
        hidden[layer] = fresh.astype(BF)
        for o in others:
            ghost_copy(layer + 1, o).start()
        ghost[layer + 1, SELF] = fresh.astype(BF)

    def project(layer):
        both = jnp.concatenate([wr_ref[layer], wl_ref[layer]], axis=1)

        got = dot(ghost[layer].reshape(OFFSETS * ATOMS, 128), both).astype(BF)
        for o in range(OFFSETS):
            tables[o, 0:64, 0:128] = got[o * 64 : (o + 1) * 64, :128]
            tables[o, 64:128, 128:256] = got[o * 64 : (o + 1) * 64, 128:]

    def twice(w):
        none = jnp.zeros_like(w)
        return jnp.concatenate(
            [jnp.concatenate([w, none], axis=1), jnp.concatenate([none, w], axis=1)], axis=0
        )

    averages = twice(jnp.full((128, 128), 1.0 / 128.0, BF))

    def edge_layer(layer, final):
        right = tables[SELF, 0:64, 0:128].astype(F32)
        left = tables[SELF, 64:128, 128:256].astype(F32)
        near = jnp.concatenate([left, right], axis=1)
        near = jnp.concatenate([near, near] * GROUP, axis=0)
        edge_in, edge_out = twice(wi_ref[layer]), twice(wo_ref[layer])

        def one(step, carry):
            state = edge[pl.ds(step * GROUP, GROUP)].reshape(GROUP * 128, 256)
            inner = dot(state, edge_in)
            reached = [
                dot(pick_far[step * GROUP + i], tables[step * GROUP + i]) for i in range(GROUP)
            ]
            product = jnp.concatenate(reached, axis=0) * near
            gate = silu(inner * product).astype(BF)
            renewed = state.astype(F32) + dot(gate, edge_out)
            mean = dot((renewed * renewed).astype(BF), averages)
            fresh = renewed * lax.rsqrt(mean + 1e-06)
            if final:
                for i in range(GROUP):
                    at = (step * GROUP + i) * 256
                    last[pl.ds(at, 128), :] = fresh[i * 128 : (i + 1) * 128, :128]
                    last[pl.ds(at + 128, 128), :] = fresh[i * 128 : (i + 1) * 128, 128:]
            else:
                edge[pl.ds(step * GROUP, GROUP)] = fresh.astype(BF).reshape(GROUP, 128, 256)
            return carry

        lax.fori_loop(0, OFFSETS // GROUP, one, 0, unroll=UNROLL)

    subq = sub.astype(F32)

    def own_step(o, carry):
        picker = jnp.where(rows[2, pl.ds(o, 1), :] == subq, 1.0, 0.0).astype(BF).T
        edge[o, :, 0:128] = dot(picker, bond_send[o]).astype(BF)
        return carry

    lax.fori_loop(0, OFFSETS, own_step, 0, unroll=6)

    atom_lane = ((lax.broadcasted_iota(jnp.int32, (NEIGH, 128), 1) & 63) * NEIGH - 1).astype(F32)
    column = jnp.where(where_to > 0.0, where_to + atom_lane, -1.0)
    column = jnp.concatenate([column, jnp.full((128 - NEIGH, 128), -1.0, F32)], axis=0).T
    column = pltpu.roll(column, 0, 1, stride=NEIGH - 64, stride_axis=0)
    column = jnp.where((sub & 1) == 1, pltpu.roll(column, 64, 1), column)
    for c in range(SLOTS // 128):
        first, final = c * 128 // NEIGH, (c * 128 + 127) // NEIGH
        found = column[first : first + 1, :]
        for n in range(first + 1, final + 1):
            found = jnp.where(lane1 >= n * NEIGH - c * 128, column[n : n + 1, :], found)
        flat[c : c + 1, :] = found

    def place_step(i, carry):
        base = i // 9 * (SLOTS // 2)
        start = base + jnp.clip(i % 9 * 256 - 128, 0, SLOTS // 2 - 512)
        here = (lax.broadcasted_iota(jnp.int32, (512, 128), 0) + start).astype(F32)
        for k in range(2):
            wanted = flat[pl.ds(2 * i + k, 1), :]
            place[i, :, k * 128 : (k + 1) * 128] = jnp.where(here == wanted, 1.0, 0.0).astype(BF)
        return carry

    lax.fori_loop(0, SLOTS // 256, place_step, 0)

    tables[...] = jnp.zeros_like(tables)
    for i in (12, 13, 14):
        fetches[i].wait()
    wait_ghost(0)
    update_hidden(0)

    for i in (8, 9, 10, 11, 15):
        fetches[i].wait()
    project(0)
    for o in others:
        pltpu.make_async_remote_copy(
            src_ref=bond_recv.at[o],
            dst_ref=bond_recv.at[o],
            send_sem=send_sem.at[3, o],
            recv_sem=recv_sem.at[3, o],
            device_id=partner(o),
            device_id_type=MESH,
        ).wait_recv()
    bond_recv[SELF] = bond_send[SELF]

    def recv_step(o, carry):
        picker = jnp.where(rows[3, pl.ds(o, 1), :] == subq, 1.0, 0.0).astype(BF).T
        edge[o, :, 128:256] = dot(picker, bond_recv[o]).astype(BF)
        return carry

    lax.fori_loop(0, OFFSETS, recv_step, 0, unroll=6)
    edge_layer(0, False)

    wait_ghost(1)
    update_hidden(1)
    project(1)
    edge_layer(1, False)

    row = lax.broadcasted_iota(jnp.int32, (ORB * ORB, ORB * ORB), 0)
    col = lax.broadcasted_iota(jnp.int32, (ORB * ORB, ORB * ORB), 1)
    coarse = jnp.floor((row.astype(F32) + 0.5) * (1.0 / ORB))
    source = (row.astype(F32) - coarse * ORB) * ORB + coarse
    swap = jnp.where(source == col.astype(F32), 1.0, 0.0).astype(BF)
    block_map = jnp.concatenate([wb_ref[...], dot(swap, wb_ref[...]).astype(BF)], axis=1)

    wait_ghost(2)
    project(2)
    edge_layer(2, True)

    is_own = (lax.broadcasted_iota(jnp.int32, (128, 128), 1) & 2) == 0
    half = SLOTS // 2

    def gather_half(h):
        for m in range(h * 16, h * 16 + 16):
            mine = [last[pl.ds(2 * m + i, NEIGH, stride=ATOMS), :] for i in range(2)]
            wide[m * 144 : m * 144 + 144, :] = jnp.concatenate(mine, axis=0).astype(BF)
        for c in range(h * 18, h * 18 + 18):
            at = c * 128
            mine = wide[at : at + 128, :].T.astype(F32)
            turned[0:128, at : at + 128] = jnp.where(is_own, mine, 0.0).astype(BF)
            turned[128:256, at : at + 128] = jnp.where(is_own, 0.0, mine).astype(BF)

    def block_half(h):
        for c in range(3):
            at = h * half + c * 768
            blocks[:, at : at + 768] = dot(block_map, turned[:, at : at + 768]).astype(BF)

    def out_half(h):
        for i in range(9):
            start = h * half + min(max(i * 256 - 128, 0), half - 512)
            at = h * half + i * 256
            out_ref[:, at : at + 256] = dot(
                blocks[:, start : start + 512], place[h * 9 + i]
            ).astype(BF)

    gather_half(0)
    block_half(0)
    gather_half(1)
    out_half(0)
    block_half(1)
    out_half(1)

    for layer in range(LAYERS):
        for o in others:
            ghost_copy(layer, o).wait_send()
    for o in others:
        bond_copy(o).wait_send()


def shards(
    atom_feats,
    bond_embed,
    pair_dist,
    neighbours,
    slot_kind,
    own_rows,
    send_pos,
    recv_pos,
    w_left,
    w_right,
    w_edge_in,
    w_edge_out,
    w_msg,
    w_upd,
    node_gain,
    w_block,
):
    hbm, vmem = pl.BlockSpec(memory_space=pltpu.HBM), pl.BlockSpec(memory_space=pltpu.VMEM)
    operands = (
        atom_feats,
        bond_embed,
        pair_dist.reshape(SLOTS // 128, 128),
        neighbours.reshape(SLOTS // 128, 128),
        slot_kind.reshape(SLOTS // 128, 128),
        own_rows.reshape(OFFSETS, 128),
        send_pos.reshape(OFFSETS, 128),
        recv_pos.reshape(SLOTS // 128, 128),
        w_left,
        w_right,
        w_edge_in,
        w_edge_out,
        w_msg,
        w_upd,
        node_gain,
        w_block.T,
    )
    return pl.pallas_call(
        kernel,
        out_shape=jax.ShapeDtypeStruct((ORB * ORB, SLOTS), BF),
        in_specs=[hbm] * len(operands),
        out_specs=vmem,
        scratch_shapes=[pltpu.VMEM(v.shape, v.dtype) for v in operands]
        + [
            pltpu.VMEM((LAYERS, OFFSETS, ATOMS, 128), BF),
            pltpu.VMEM((LAYERS - 1, ATOMS, 128), BF),
            pltpu.VMEM((OFFSETS, CAP, 128), BF),
            pltpu.VMEM((OFFSETS, CAP, 128), BF),
            pltpu.VMEM((2, ATOMS, 128), F32),
            pltpu.VMEM((6, 24, 128), F32),
            pltpu.VMEM((40, 128), F32),
            pltpu.VMEM((OFFSETS, 128, 128), BF),
            pltpu.VMEM((128, OFFSETS * ATOMS), BF),
            pltpu.VMEM((OFFSETS, 128, 256), BF),
            pltpu.VMEM((OFFSETS, 128, 256), BF),
            pltpu.VMEM((SLOTS, 128), F32),
            pltpu.VMEM((SLOTS, 128), BF),
            pltpu.VMEM((256, SLOTS), BF),
            pltpu.VMEM((SLOTS // 256, 512, 256), BF),
            pltpu.VMEM((ORB * ORB, SLOTS), BF),
            pltpu.SemaphoreType.DMA((len(operands),)),
            pltpu.SemaphoreType.DMA((1,)),
            pltpu.SemaphoreType.DMA((4, OFFSETS)),
            pltpu.SemaphoreType.DMA((4, OFFSETS)),
        ],
        compiler_params=pltpu.CompilerParams(
            collective_id=0, has_side_effects=True, vmem_limit_bytes=60 << 20
        ),
    )(*operands)


def solution(mesh):
    spread = ("gx", "gy", "layer")
    placed = (P(spread, None), P(spread, None)) + (P(spread),) * 6 + (P(),) * 8
    return jax.shard_map(
        shards, mesh=mesh, in_specs=placed, out_specs=P(None, spread), check_vma=False
    )
```

time: 83.8 us -> 43.5 us (0.52)
  Pallas kernels: 70.5 us -> 40.7 us
  local copies, waits for them, and re-layouts: 11.1 us -> 2.69 us
  other arithmetic: 1.51 us -> 0 us
    pallas_call x1, Pallas kernels: 70.5 us -> 40.7 us  [shards(): pl.pallas_call(kernel, out_shape=jax.ShapeDtypeStruct((ORB * ORB, SLOTS),...]
    unnamed x20 -> x1, local copies, waits for them, and re-layouts: 9.75 us -> 2.69 us
    reshape x2 -> x0, local copies, waits for them, and re-layouts: 0.9 us -> none  [the longest x1 0.82 us: shards(): dist = jnp.tile(pair_dist.reshape(ATOMS, NEIGH).T, (1, 2))]
where the time goes in v1:
time: 43.5 us; the launch traced here: 43.4 us
  Pallas kernels  40.7 us (94%)
  local copies, waits for them, and re-layouts  2.69 us (6%)
    pallas_call x1, Pallas kernels, shards(): pl.pallas_call(kernel, out_shape=jax.ShapeDtypeStruct((ORB * ORB, SLOTS),...  40.7 us
    unnamed x1, local copies, waits for them, and re-layouts  2.69 us

profile of v1, /device:TPU:1, one launch (start us, length us, event | category | flops | bytes accessed | tf_op | source)
XLA Modules:
  0.0 43.4 jit_solution(4135847298574495051)
XLA Ops:
  0.0 40.7 %shard_map.154 = bf16[169,4608]{1,0:T(8,128)(2,1)} custom-call(bf16[64,128]{1,0:T(8,128)(2,1)} %refs_0_.1, bf16[2304,128]{1,0:T(8,128)(2,1)} %refs_1_.1, f32[36,128]{1,0:T(8,128)} %bitcast.8, s32[36,128]{1,0:T(8,128)} %bitcast.9, s32[36,128]{1,0:T(8,128)} %bitcast.10, s32[18,128]{1,0:T(8,128)} %bitcast.12, s32[18,128]{1,0:T(8,128)} %bitcast.13, ...), custom_call_target="tpu_custom_call" | custom-call | tf_op jit(solution)/shard_map/pallas_call | solution.py:473
  40.7 2.7 %copy.18 = bf16[169,4608]{1,0:T(8,128)(2,1)} copy(bf16[169,4608]{1,0:T(8,128)(2,1)} %shard_map.154) | data formatting | bytes 3115008

commit v2 on v1

--- a/solution.py
+++ b/solution.py
@@ -14,8 +14,6 @@
 SLOTS = ATOMS * NEIGH
 CAP = 128
 LISTED = 2176
-GROUP = 3
-UNROLL = 1
 MESH = pl.DeviceIdType.MESH
 BF = jnp.bfloat16
 F32 = jnp.float32
@@ -57,9 +55,9 @@
         edge,
         last,
         wide,
-        turned,
+        spread,
         place,
-        blocks,
+        result,
         in_sem,
         out_sem,
         send_sem,
@@ -111,8 +109,8 @@
         return pltpu.make_async_remote_copy(
             src_ref=source,
             dst_ref=ghost.at[layer, reverse_of(o)],
-            send_sem=send_sem.at[layer, o],
-            recv_sem=recv_sem.at[layer, reverse_of(o)],
+            send_sem=send_sem.at[layer],
+            recv_sem=recv_sem.at[layer],
             device_id=partner(o),
             device_id_type=MESH,
         )
@@ -121,8 +119,8 @@
         return pltpu.make_async_remote_copy(
             src_ref=bond_send.at[o],
             dst_ref=bond_recv.at[reverse_of(o)],
-            send_sem=send_sem.at[3, o],
-            recv_sem=recv_sem.at[3, reverse_of(o)],
+            send_sem=send_sem.at[3],
+            recv_sem=recv_sem.at[3],
             device_id=partner(o),
             device_id_type=MESH,
         )
@@ -249,16 +247,20 @@
     fetches[1].wait()
     lax.fori_loop(0, OFFSETS // 3, bond_step, 0)
 
+    def exchange(k):
+        mine = bond_recv if k == 3 else ghost.at[k]
+        whole = mine.at[pl.ds(0, len(others))]
+        return pltpu.make_async_remote_copy(
+            src_ref=whole,
+            dst_ref=whole,
+            send_sem=send_sem.at[k],
+            recv_sem=recv_sem.at[k],
+            device_id=partner(0),
+            device_id_type=MESH,
+        )
+
     def wait_ghost(layer):
-        for o in others:
-            pltpu.make_async_remote_copy(
-                src_ref=ghost.at[layer, o],
-                dst_ref=ghost.at[layer, o],
-                send_sem=send_sem.at[layer, o],
-                recv_sem=recv_sem.at[layer, o],
-                device_id=partner(o),
-                device_id_type=MESH,
-            ).wait_recv()
+        exchange(layer).wait_recv()
 
     def update_hidden(layer):
         two = dot(mix[...], ghost[layer].reshape(OFFSETS * ATOMS, 128))
@@ -288,34 +290,27 @@
 
     averages = twice(jnp.full((128, 128), 1.0 / 128.0, BF))
 
-    def edge_layer(layer, final):
+    def edge_inner(layer):
+        return dot(edge[...].reshape(OFFSETS * 128, 256), twice(wi_ref[layer]))
+
+    def edge_layer(layer, final, inner):
         right = tables[SELF, 0:64, 0:128].astype(F32)
         left = tables[SELF, 64:128, 128:256].astype(F32)
         near = jnp.concatenate([left, right], axis=1)
-        near = jnp.concatenate([near, near] * GROUP, axis=0)
-        edge_in, edge_out = twice(wi_ref[layer]), twice(wo_ref[layer])
-
-        def one(step, carry):
-            state = edge[pl.ds(step * GROUP, GROUP)].reshape(GROUP * 128, 256)
-            inner = dot(state, edge_in)
-            reached = [
-                dot(pick_far[step * GROUP + i], tables[step * GROUP + i]) for i in range(GROUP)
-            ]
-            product = jnp.concatenate(reached, axis=0) * near
-            gate = silu(inner * product).astype(BF)
-            renewed = state.astype(F32) + dot(gate, edge_out)
-            mean = dot((renewed * renewed).astype(BF), averages)
-            fresh = renewed * lax.rsqrt(mean + 1e-06)
-            if final:
-                for i in range(GROUP):
-                    at = (step * GROUP + i) * 256
-                    last[pl.ds(at, 128), :] = fresh[i * 128 : (i + 1) * 128, :128]
-                    last[pl.ds(at + 128, 128), :] = fresh[i * 128 : (i + 1) * 128, 128:]
-            else:
-                edge[pl.ds(step * GROUP, GROUP)] = fresh.astype(BF).reshape(GROUP, 128, 256)
-            return carry
-
-        lax.fori_loop(0, OFFSETS // GROUP, one, 0, unroll=UNROLL)
+        near = jnp.concatenate([near, near] * OFFSETS, axis=0)
+        state = edge[...].reshape(OFFSETS * 128, 256)
+        reached = [dot(pick_far[o], tables[o]) for o in range(OFFSETS)]
+        gate = silu(inner * (jnp.concatenate(reached, axis=0) * near)).astype(BF)
+        renewed = state.astype(F32) + dot(gate, twice(wo_ref[layer]))
+        mean = dot((renewed * renewed).astype(BF), averages)
+        fresh = renewed * lax.rsqrt(mean + 1e-06)
+        if final:
+            for o in range(OFFSETS):
+                mine = fresh[o * 128 : (o + 1) * 128, :]
+                last[o * 256 : o * 256 + 128, :] = mine[:, :128]
+                last[o * 256 + 128 : o * 256 + 256, :] = mine[:, 128:]
+        else:
+            edge[...] = fresh.astype(BF).reshape(OFFSETS, 128, 256)
 
     subq = sub.astype(F32)
 
@@ -326,28 +321,23 @@
 
     lax.fori_loop(0, OFFSETS, own_step, 0, unroll=6)
 
-    atom_lane = ((lax.broadcasted_iota(jnp.int32, (NEIGH, 128), 1) & 63) * NEIGH - 1).astype(F32)
-    column = jnp.where(where_to > 0.0, where_to + atom_lane, -1.0)
-    column = jnp.concatenate([column, jnp.full((128 - NEIGH, 128), -1.0, F32)], axis=0).T
-    column = pltpu.roll(column, 0, 1, stride=NEIGH - 64, stride_axis=0)
-    column = jnp.where((sub & 1) == 1, pltpu.roll(column, 64, 1), column)
-    for c in range(SLOTS // 128):
-        first, final = c * 128 // NEIGH, (c * 128 + 127) // NEIGH
-        found = column[first : first + 1, :]
-        for n in range(first + 1, final + 1):
-            found = jnp.where(lane1 >= n * NEIGH - c * 128, column[n : n + 1, :], found)
-        flat[c : c + 1, :] = found
+    for n in range(ATOMS):
+        place_of = jnp.broadcast_to(where_to[:, n : n + 1], (NEIGH, 128))
+        spread[n * NEIGH : (n + 1) * NEIGH, :] = jnp.where(
+            place_of > 0.0, place_of + (n % 32 * NEIGH - 1.0), -1.0
+        )
 
     def place_step(i, carry):
-        base = i // 9 * (SLOTS // 2)
-        start = base + jnp.clip(i % 9 * 256 - 128, 0, SLOTS // 2 - 512)
-        here = (lax.broadcasted_iota(jnp.int32, (512, 128), 0) + start).astype(F32)
-        for k in range(2):
-            wanted = flat[pl.ds(2 * i + k, 1), :]
-            place[i, :, k * 128 : (k + 1) * 128] = jnp.where(here == wanted, 1.0, 0.0).astype(BF)
+        start = jnp.clip(i % 9 * 256 - 128, 0, SLOTS // 2 - 512)
+        wanted = spread[pl.ds(pl.multiple_of(i * 256, 256), 256), :]
+        for k in range(4):
+            here = lax.broadcasted_iota(jnp.int32, (256, 128), 1) + (start + k * 128)
+            place[i, :, k * 128 : (k + 1) * 128] = jnp.where(
+                wanted == here.astype(F32), 1.0, 0.0
+            ).astype(BF)
         return carry
 
-    lax.fori_loop(0, SLOTS // 256, place_step, 0)
+    lax.fori_loop(0, SLOTS // 256, place_step, 0, unroll=2)
 
     tables[...] = jnp.zeros_like(tables)
     for i in (12, 13, 14):
@@ -358,15 +348,10 @@
     for i in (8, 9, 10, 11, 15):
         fetches[i].wait()
     project(0)
-    for o in others:
-        pltpu.make_async_remote_copy(
-            src_ref=bond_recv.at[o],
-            dst_ref=bond_recv.at[o],
-            send_sem=send_sem.at[3, o],
-            recv_sem=recv_sem.at[3, o],
-            device_id=partner(o),
-            device_id_type=MESH,
-        ).wait_recv()
+    wait_ghost(1)
+    update_hidden(1)
+
+    exchange(3).wait_recv()
     bond_recv[SELF] = bond_send[SELF]
 
     def recv_step(o, carry):
@@ -375,12 +360,11 @@
         return carry
 
     lax.fori_loop(0, OFFSETS, recv_step, 0, unroll=6)
-    edge_layer(0, False)
-
-    wait_ghost(1)
-    update_hidden(1)
+    edge_layer(0, False, edge_inner(0))
+
     project(1)
-    edge_layer(1, False)
+    edge_layer(1, False, edge_inner(1))
+    inner = edge_inner(2)
 
     row = lax.broadcasted_iota(jnp.int32, (ORB * ORB, ORB * ORB), 0)
     col = lax.broadcasted_iota(jnp.int32, (ORB * ORB, ORB * ORB), 1)
@@ -391,46 +375,39 @@
 
     wait_ghost(2)
     project(2)
-    edge_layer(2, True)
-
-    is_own = (lax.broadcasted_iota(jnp.int32, (128, 128), 1) & 2) == 0
+    edge_layer(2, True, inner)
+
     half = SLOTS // 2
 
-    def gather_half(h):
+    def write(c):
+        columns = pl.ds(c * 768, 768)
+        return pltpu.make_async_copy(
+            result.at[:, columns], out_ref.at[:, columns], out_sem.at[c]
+        )
+
+    for h in range(2):
         for m in range(h * 16, h * 16 + 16):
             mine = [last[pl.ds(2 * m + i, NEIGH, stride=ATOMS), :] for i in range(2)]
             wide[m * 144 : m * 144 + 144, :] = jnp.concatenate(mine, axis=0).astype(BF)
-        for c in range(h * 18, h * 18 + 18):
-            at = c * 128
-            mine = wide[at : at + 128, :].T.astype(F32)
-            turned[0:128, at : at + 128] = jnp.where(is_own, mine, 0.0).astype(BF)
-            turned[128:256, at : at + 128] = jnp.where(is_own, 0.0, mine).astype(BF)
-
-    def block_half(h):
-        for c in range(3):
-            at = h * half + c * 768
-            blocks[:, at : at + 768] = dot(block_map, turned[:, at : at + 768]).astype(BF)
-
-    def out_half(h):
+    for h in range(2):
+        states = []
         for i in range(9):
             start = h * half + min(max(i * 256 - 128, 0), half - 512)
+            states.append(dot(place[h * 9 + i], wide[start : start + 512, :]).astype(BF).T)
+        for i in range(9):
             at = h * half + i * 256
-            out_ref[:, at : at + 256] = dot(
-                blocks[:, start : start + 512], place[h * 9 + i]
-            ).astype(BF)
-
-    gather_half(0)
-    block_half(0)
-    gather_half(1)
-    out_half(0)
-    block_half(1)
-    out_half(1)
-
-    for layer in range(LAYERS):
-        for o in others:
-            ghost_copy(layer, o).wait_send()
-    for o in others:
-        bond_copy(o).wait_send()
+            kinds = [kind_ref[at // 128 + k : at // 128 + k + 1, :] for k in range(2)]
+            kinds = jnp.concatenate(kinds, axis=1)
+            state = states[i].astype(F32)
+            stacked = [jnp.where(kinds == k, state, 0.0).astype(BF) for k in (1, 2)]
+            result[:, at : at + 256] = dot(block_map, jnp.concatenate(stacked, axis=0)).astype(BF)
+            if i % 3 == 2:
+                write(h * 3 + i // 3).start()
+
+    for c in range(6):
+        write(c).wait()
+    for k in range(4):
+        exchange(k).wait_send()
 
 
 def shards(
@@ -451,7 +428,7 @@
     node_gain,
     w_block,
 ):
-    hbm, vmem = pl.BlockSpec(memory_space=pltpu.HBM), pl.BlockSpec(memory_space=pltpu.VMEM)
+    hbm = pl.BlockSpec(memory_space=pltpu.HBM)
     operands = (
         atom_feats,
         bond_embed,
@@ -474,7 +451,7 @@
         kernel,
         out_shape=jax.ShapeDtypeStruct((ORB * ORB, SLOTS), BF),
         in_specs=[hbm] * len(operands),
-        out_specs=vmem,
+        out_specs=hbm,
         scratch_shapes=[pltpu.VMEM(v.shape, v.dtype) for v in operands]
         + [
             pltpu.VMEM((LAYERS, OFFSETS, ATOMS, 128), BF),
@@ -490,13 +467,13 @@
             pltpu.VMEM((OFFSETS, 128, 256), BF),
             pltpu.VMEM((SLOTS, 128), F32),
             pltpu.VMEM((SLOTS, 128), BF),
-            pltpu.VMEM((256, SLOTS), BF),
-            pltpu.VMEM((SLOTS // 256, 512, 256), BF),
+            pltpu.VMEM((SLOTS, 128), F32),
+            pltpu.VMEM((SLOTS // 256, 256, 512), BF),
             pltpu.VMEM((ORB * ORB, SLOTS), BF),
             pltpu.SemaphoreType.DMA((len(operands),)),
-            pltpu.SemaphoreType.DMA((1,)),
-            pltpu.SemaphoreType.DMA((4, OFFSETS)),
-            pltpu.SemaphoreType.DMA((4, OFFSETS)),
+            pltpu.SemaphoreType.DMA((6,)),
+            pltpu.SemaphoreType.DMA((4,)),
+            pltpu.SemaphoreType.DMA((4,)),
         ],
         compiler_params=pltpu.CompilerParams(
             collective_id=0, has_side_effects=True, vmem_limit_bytes=60 << 20

time: 43.5 us -> 38.8 us (0.89)
  Pallas kernels: 40.7 us -> 35.9 us
    pallas_call x1, Pallas kernels: 40.7 us -> 35.9 us  [shards(): pl.pallas_call(kernel, out_shape=jax.ShapeDtypeStruct((ORB * ORB, SLOTS),...]
where the time goes in v2:
time: 38.8 us; the launch traced here: 38.6 us
  Pallas kernels  35.9 us (93%)
  local copies, waits for them, and re-layouts  2.69 us (7%)
    pallas_call x1, Pallas kernels, shards(): pl.pallas_call(kernel, out_shape=jax.ShapeDtypeStruct((ORB * ORB, SLOTS),...  35.9 us
    unnamed x1, local copies, waits for them, and re-layouts  2.69 us

profile of v2, /device:TPU:1, one launch (start us, length us, event | category | flops | bytes accessed | tf_op | source)
XLA Modules:
  0.0 38.6 jit_solution(1254372104503735490)
XLA Ops:
  0.0 35.9 %shard_map.154 = bf16[169,4608]{1,0:T(8,128)(2,1)} custom-call(bf16[64,128]{1,0:T(8,128)(2,1)} %refs_0_.1, bf16[2304,128]{1,0:T(8,128)(2,1)} %refs_1_.1, f32[36,128]{1,0:T(8,128)} %bitcast.8, s32[36,128]{1,0:T(8,128)} %bitcast.9, s32[36,128]{1,0:T(8,128)} %bitcast.10, s32[18,128]{1,0:T(8,128)} %bitcast.12, s32[18,128]{1,0:T(8,128)} %bitcast.13, ...), custom_call_target="tpu_custom_call" | custom-call | tf_op jit(solution)/shard_map/pallas_call | solution.py:450
  35.9 2.7 %copy.18 = bf16[169,4608]{1,0:T(8,128)(2,1)} copy(bf16[169,4608]{1,0:T(8,128)(2,1)} %shard_map.154) | data formatting | bytes 3115008

commit v3 on v2

--- a/solution.py
+++ b/solution.py
@@ -157,67 +157,6 @@
     recv_place = (place_in + 1).astype(F32)
 
     sub72 = lax.broadcasted_iota(jnp.int32, (NEIGH, 128), 0)
-    send_place = jnp.zeros((NEIGH, 128), F32)
-    own_rows = own_ref[...].astype(F32)
-    own_atom = jnp.floor((own_rows + 0.5) * (1.0 / NEIGH))
-    own_slot = own_rows - own_atom * NEIGH
-    own_place = ((send_ref[...] & 127) + 1).astype(F32)
-    sub_slot, sub_atom = sub72.astype(F32), (sub & 63).astype(F32)
-    for k in range(OFFSETS):
-        at_slot = jnp.where(own_slot[k : k + 1, :] == sub_slot, 1.0, 0.0).astype(BF)
-        at_atom = jnp.where(own_atom[k : k + 1, :] == sub_atom, own_place[k : k + 1, :], 0.0)
-        send_place = send_place + dot_nt(at_slot, at_atom.astype(BF))
-
-    before = jnp.where(
-        lax.broadcasted_iota(jnp.int32, (NEIGH, NEIGH), 0)
-        > lax.broadcasted_iota(jnp.int32, (NEIGH, NEIGH), 1),
-        1.0,
-        0.0,
-    ).astype(BF)
-    rank_lane = (lax.broadcasted_iota(jnp.int32, (NEIGH, 128), 1) >> 6).astype(F32)
-
-    def total(v):
-        return jnp.sum(v, axis=0, keepdims=True)
-
-    def tables_step(o, where_to):
-        own = jnp.where(own_key == o, 1.0, 0.0)
-        far = jnp.where(far_key == o, 1.0, 0.0)
-        count = dot(before, jnp.concatenate([own, far], axis=1).astype(BF))
-        own_rank, far_rank = count[:, :128], count[:, 128:]
-        own_hit = jnp.where(own_rank == rank_lane, own, 0.0)
-        far_hit = jnp.where(far_rank == rank_lane, far, 0.0)
-        rows[0, pl.ds(o, 1), :] = total(own_hit * atom_of) - 1.0
-        rows[1, pl.ds(o, 1), :] = total(far_hit * atom_of) - 1.0
-        rows[2, pl.ds(o, 1), :] = total(own_hit * send_place) - 1.0
-        rows[3, pl.ds(o, 1), :] = total(far_hit * recv_place) - 1.0
-        rows[4, pl.ds(o, 1), :] = total(own_hit * env)
-        rows[5, pl.ds(o, 1), :] = total(far_hit * env)
-        base = (4 * o + 1).astype(F32)
-        return where_to + own * (own_rank + base) + far * (far_rank + (base + 2.0))
-
-    where_to = lax.fori_loop(0, OFFSETS, tables_step, jnp.zeros((NEIGH, 128), F32), unroll=6)
-
-    subf = (sub & 63).astype(F32)
-    for g in range(OFFSETS // 2):
-        low = sub < 64
-
-        def pair(kind_of_row):
-            first = rows[kind_of_row, 2 * g : 2 * g + 1, :]
-            second = rows[kind_of_row, 2 * g + 1 : 2 * g + 2, :]
-            return jnp.where(low, first, second)
-
-        weights = jnp.where(pair(0) == subf, pair(4), 0.0) + jnp.where(
-            pair(1) == subf, pair(5), 0.0
-        )
-        mix[:, g * 128 : (g + 1) * 128] = weights.T.astype(BF)
-
-    def far_step(o, carry):
-        own_atom, far_atom = rows[0, pl.ds(o, 1), :], rows[1, pl.ds(o, 1), :]
-        wanted = jnp.where(sub < 64, own_atom, far_atom)
-        pick_far[o] = jnp.where(wanted == subf, 1.0, 0.0).astype(BF).T
-        return carry
-
-    lax.fori_loop(0, OFFSETS, far_step, 0, unroll=6)
     fetches[0].wait()
 
     pl.semaphore_wait(barrier, len(others))
@@ -312,6 +251,67 @@
         else:
             edge[...] = fresh.astype(BF).reshape(OFFSETS, 128, 256)
 
+    send_place = jnp.zeros((NEIGH, 128), F32)
+    own_rows = own_ref[...].astype(F32)
+    own_atom = jnp.floor((own_rows + 0.5) * (1.0 / NEIGH))
+    own_slot = own_rows - own_atom * NEIGH
+    own_place = ((send_ref[...] & 127) + 1).astype(F32)
+    sub_slot, sub_atom = sub72.astype(F32), (sub & 63).astype(F32)
+    for k in range(OFFSETS):
+        at_slot = jnp.where(own_slot[k : k + 1, :] == sub_slot, 1.0, 0.0).astype(BF)
+        at_atom = jnp.where(own_atom[k : k + 1, :] == sub_atom, own_place[k : k + 1, :], 0.0)
+        send_place = send_place + dot_nt(at_slot, at_atom.astype(BF))
+
+    before = jnp.where(
+        lax.broadcasted_iota(jnp.int32, (NEIGH, NEIGH), 0)
+        > lax.broadcasted_iota(jnp.int32, (NEIGH, NEIGH), 1),
+        1.0,
+        0.0,
+    ).astype(BF)
+    rank_lane = (lax.broadcasted_iota(jnp.int32, (NEIGH, 128), 1) >> 6).astype(F32)
+
+    def total(v):
+        return jnp.sum(v, axis=0, keepdims=True)
+
+    def tables_step(o, where_to):
+        own = jnp.where(own_key == o, 1.0, 0.0)
+        far = jnp.where(far_key == o, 1.0, 0.0)
+        count = dot(before, jnp.concatenate([own, far], axis=1).astype(BF))
+        own_rank, far_rank = count[:, :128], count[:, 128:]
+        own_hit = jnp.where(own_rank == rank_lane, own, 0.0)
+        far_hit = jnp.where(far_rank == rank_lane, far, 0.0)
+        rows[0, pl.ds(o, 1), :] = total(own_hit * atom_of) - 1.0
+        rows[1, pl.ds(o, 1), :] = total(far_hit * atom_of) - 1.0
+        rows[2, pl.ds(o, 1), :] = total(own_hit * send_place) - 1.0
+        rows[3, pl.ds(o, 1), :] = total(far_hit * recv_place) - 1.0
+        rows[4, pl.ds(o, 1), :] = total(own_hit * env)
+        rows[5, pl.ds(o, 1), :] = total(far_hit * env)
+        base = (4 * o + 1).astype(F32)
+        return where_to + own * (own_rank + base) + far * (far_rank + (base + 2.0))
+
+    where_to = lax.fori_loop(0, OFFSETS, tables_step, jnp.zeros((NEIGH, 128), F32), unroll=6)
+
+    subf = (sub & 63).astype(F32)
+    for g in range(OFFSETS // 2):
+        low = sub < 64
+
+        def pair(kind_of_row):
+            first = rows[kind_of_row, 2 * g : 2 * g + 1, :]
+            second = rows[kind_of_row, 2 * g + 1 : 2 * g + 2, :]
+            return jnp.where(low, first, second)
+
+        weights = jnp.where(pair(0) == subf, pair(4), 0.0) + jnp.where(
+            pair(1) == subf, pair(5), 0.0
+        )
+        mix[:, g * 128 : (g + 1) * 128] = weights.T.astype(BF)
+
+    def far_step(o, carry):
+        own_atom, far_atom = rows[0, pl.ds(o, 1), :], rows[1, pl.ds(o, 1), :]
+        wanted = jnp.where(sub < 64, own_atom, far_atom)
+        pick_far[o] = jnp.where(wanted == subf, 1.0, 0.0).astype(BF).T
+        return carry
+
+    lax.fori_loop(0, OFFSETS, far_step, 0, unroll=6)
     subq = sub.astype(F32)
 
     def own_step(o, carry):
@@ -398,8 +398,7 @@
             at = h * half + i * 256
             kinds = [kind_ref[at // 128 + k : at // 128 + k + 1, :] for k in range(2)]
             kinds = jnp.concatenate(kinds, axis=1)
-            state = states[i].astype(F32)
-            stacked = [jnp.where(kinds == k, state, 0.0).astype(BF) for k in (1, 2)]
+            stacked = [jnp.where(kinds == k, 1.0, 0.0).astype(BF) * states[i] for k in (1, 2)]
             result[:, at : at + 256] = dot(block_map, jnp.concatenate(stacked, axis=0)).astype(BF)
             if i % 3 == 2:
                 write(h * 3 + i // 3).start()

time: 38.8 us -> 38.2 us (0.985)
  Pallas kernels: 35.9 us -> 35.3 us
    pallas_call x1, Pallas kernels: 35.9 us -> 35.3 us  [shards(): pl.pallas_call(kernel, out_shape=jax.ShapeDtypeStruct((ORB * ORB, SLOTS),...]
where the time goes in v3:
time: 38.2 us; the launch traced here: 38 us
  Pallas kernels  35.3 us (92%)
  local copies, waits for them, and re-layouts  2.69 us (7%)
    pallas_call x1, Pallas kernels, shards(): pl.pallas_call(kernel, out_shape=jax.ShapeDtypeStruct((ORB * ORB, SLOTS),...  35.3 us
    unnamed x1, local copies, waits for them, and re-layouts  2.69 us

profile of v3, /device:TPU:1, one launch (start us, length us, event | category | flops | bytes accessed | tf_op | source)
XLA Modules:
  0.0 38.0 jit_solution(9717865632160004278)
XLA Ops:
  0.0 35.3 %shard_map.154 = bf16[169,4608]{1,0:T(8,128)(2,1)} custom-call(bf16[64,128]{1,0:T(8,128)(2,1)} %refs_0_.1, bf16[2304,128]{1,0:T(8,128)(2,1)} %refs_1_.1, f32[36,128]{1,0:T(8,128)} %bitcast.8, s32[36,128]{1,0:T(8,128)} %bitcast.9, s32[36,128]{1,0:T(8,128)} %bitcast.10, s32[18,128]{1,0:T(8,128)} %bitcast.12, s32[18,128]{1,0:T(8,128)} %bitcast.13, ...), custom_call_target="tpu_custom_call" | custom-call | tf_op jit(solution)/shard_map/pallas_call | solution.py:449
  35.3 2.7 %copy.18 = bf16[169,4608]{1,0:T(8,128)(2,1)} copy(bf16[169,4608]{1,0:T(8,128)(2,1)} %shard_map.154) | data formatting | bytes 3115008
